TPU v7x, 128 devices: a whole 4x4x4 slice. The times are simulated.
128 devices in a mesh: site: 4 (over z), blk: 16 (over x, y), charge: 2 (over core).
Axes of the slice: x: 4, y: 4, z: 4, core: 2. Of those that a mesh axis runs over, the one named last changes fastest.
Arguments:
- theta: bfloat16 [4, 64, 128, 2048], P('site', ('blk', 'charge')), may hold values from -6 to 6
- boundary_env: bfloat16 [64, 18, 128, 128], P(('blk', 'charge')), may hold values from -1 to 1
- right_env: bfloat16 [4, 64, 18, 128, 128], P('site', ('blk', 'charge')), may hold values from -1 to 1
- site_tensors: bfloat16 [4, 2, 64, 4, 128, 128], P('site', None, ('blk', 'charge')), may hold values from -0.375 to 0.375
- site_mpo: bfloat16 [4, 2, 18, 18, 4, 4], P('site'), may hold values from -0.75 to 0.75
- bond_ops: bfloat16 [4, 18, 16, 16], P('site'), may hold values from -1 to 1
- block_energy: float32 [4, 64], P('site', ('blk', 'charge')), may hold values from 1 to 4
- sector_charge: int32 [4, 64], P('site', ('blk', 'charge')), may hold values from 0 to 63, as said below
- block_len: int32 [4, 64], P('site', ('blk', 'charge')), may hold values from 64 to 128
- channel_charge: int32 [18], replicated, may hold values from -1 to 1
Outputs:
- env_out: bfloat16 [4, 64, 18, 128, 128], P('site', ('blk', 'charge'))
- lanczos: bfloat16 [4, 64, 128, 2048], P('site', ('blk', 'charge'))
- coefficients: float32 [4, 2], P('site')
Inputs may be any that keep to these rules, and one draw needn't show every extreme that they name: `sector_charge`: in each section every label of 0 to 63 appears exactly once; the blocks held at index c of the charge axis carry labels of parity c.
All inputs are finite; a program needn't handle non-finite values.
Results may differ from a plain program's by a relative error of at most 0.03.
Values may be sent and summed in bfloat16 or wider, within the bound.
A program may use at most 128 MiB of HBM per device.

v0:
```python
import jax
import jax.numpy as jnp
from jax import lax
from jax.sharding import PartitionSpec as P

BS = 128
M = 2048
NS = 64


def from_behind(block, axis, distance):
    devices = range(lax.axis_size(axis))
    route = [(i - distance, i) for i in devices if i - distance in devices]
    return lax.ppermute(block, axis, route)


def from_partner(shard, axis, bit):
    return lax.ppermute(shard, axis, [(i, i ^ 1 << bit) for i in range(lax.axis_size(axis))])


def env_update(environ, tensors, site_op):

    def one_block(entries):
        env_block, site_blocks = entries
        left_part = jnp.einsum(
            "wab,sbc->wsac", env_block, site_blocks, preferred_element_type=jnp.float32
        ).astype(jnp.bfloat16)
        mixed = jnp.einsum(
            "wvts,wsac->vtac", site_op, left_part, preferred_element_type=jnp.float32
        ).astype(jnp.bfloat16)
        return jnp.einsum(
            "tab,vtac->vbc", site_blocks, mixed, preferred_element_type=jnp.float32
        ).astype(jnp.bfloat16)

    return lax.map(one_block, (environ, tensors))


def block_product(env_block, right_blocks, chosen, ops, charges):

    def segment(total_sum, entries):
        left_block, right_block, bond_op, charge = entries
        source_tile = lax.dynamic_index_in_dim(chosen, charge + 1, 0, keepdims=False)
        contracted = jnp.dot(left_block, source_tile, preferred_element_type=jnp.float32).astype(
            jnp.bfloat16
        )
        shaped = contracted.reshape(contracted.shape[0], ops.shape[1], -1)
        applied = jnp.einsum(
            "asb,bc->asc", shaped, right_block, preferred_element_type=jnp.float32
        ).astype(jnp.bfloat16)
        final = jnp.einsum("asc,st->atc", applied, bond_op, preferred_element_type=jnp.float32)
        return (total_sum + final.reshape(total_sum.shape), None)

    start_sum = jnp.zeros((chosen.shape[1], chosen.shape[2]), jnp.float32)
    return lax.scan(segment, start_sum, (env_block, right_blocks, ops, charges))[0]


def keep_same(values):
    return values


def pair_with(environ, tensors, site_ops):
    first = env_update(environ, tensors[0], site_ops[0])
    return env_update(first, tensors[1], site_ops[1])


def picker(wanted_labels, pieces):
    sign_pair = jnp.array([-1, 1], jnp.int32)
    wanted = wanted_labels[:, None] + sign_pair[None, :]
    incoming_tiles, incoming_tags = pieces
    matches = (incoming_tags[None, None, :] == wanted[:, :, None]).astype(jnp.bfloat16)
    picked = jnp.einsum(
        "kst,tam->ksam", matches, incoming_tiles, preferred_element_type=jnp.float32
    )
    return picked.astype(jnp.bfloat16)


def on_device(
    theta,
    boundary_env,
    right_env,
    site_tensors,
    site_mpo,
    bond_ops,
    block_energy,
    sector_charge,
    block_len,
    channel_charge,
):
    section = lax.axis_index("site")
    site_count = lax.axis_size("site")
    tensors = site_tensors[0]
    site_ops = site_mpo[0]

    def update_pair(environ):
        return pair_with(environ, tensors, site_ops)

    state = boundary_env
    env_in = boundary_env
    for segment in range(site_count):
        state = lax.cond(section == segment, update_pair, keep_same, state)
        if segment + 1 < site_count:
            received = from_behind(state, "site", 1)
            is_next = section == segment + 1
            state = jnp.where(is_next, received, state)
            env_in = jnp.where(is_next, received, env_in)
    labels = sector_charge[0]
    live_rows = block_len[0]
    row_mask = jnp.arange(theta.shape[2], dtype=jnp.int32)[None, :] < live_rows[:, None]
    theta_m = theta[0] * row_mask[:, :, None].astype(jnp.bfloat16)
    other_labels = from_partner(labels, "charge", 0)
    for_other = picker(
        other_labels,
        (
            lax.all_gather(theta_m, "blk", axis=0, tiled=True),
            lax.all_gather(labels, "blk", axis=0, tiled=True),
        ),
    )
    partner = from_partner(for_other, "charge", 0)
    chosen_all = jnp.stack([partner[:, 0], theta_m, partner[:, 1]], axis=1)
    ops = bond_ops[0]

    def per_block(entries):
        return block_product(entries[0], entries[1], entries[2], ops, channel_charge)

    product = lax.map(per_block, (env_in, right_env[0], chosen_all))
    theta_f = theta_m.astype(jnp.float32)
    product = (
        product * row_mask[:, :, None].astype(jnp.float32)
        - block_energy[0][:, None, None] * theta_f
    )
    entries_count = NS * BS * M
    correlation, norm_theta = lax.psum(
        (jnp.sum(theta_f * product), jnp.sum(theta_f * theta_f)), ("blk", "charge")
    )
    rayleigh = correlation / norm_theta
    residual = product - rayleigh * theta_f
    residual_sq = lax.psum(jnp.sum(residual * residual), ("blk", "charge"))
    mean_sq = residual_sq / entries_count
    lanczos = (residual / jnp.sqrt(mean_sq + 1e-06)).astype(jnp.bfloat16)
    coefficients = jnp.stack([rayleigh, jnp.sqrt(mean_sq)])[None, :]
    return (state[None], lanczos[None], coefficients)


def solution(mesh):
    return jax.shard_map(
        on_device,
        mesh=mesh,
        in_specs=(
            P("site", ("blk", "charge"), None, None),
            P(("blk", "charge"), None, None, None),
            P("site", ("blk", "charge"), None, None, None),
            P("site", None, ("blk", "charge"), None, None, None),
            P("site", None, None, None, None, None),
            P("site", None, None, None),
            P("site", ("blk", "charge")),
            P("site", ("blk", "charge")),
            P("site", ("blk", "charge")),
            P(),
        ),
        out_specs=(
            P("site", ("blk", "charge"), None, None, None),
            P("site", ("blk", "charge"), None, None),
            P("site", None),
        ),
        check_vma=False,
    )
```

profile of v0, /device:TPU:97, one launch (start us, length us, event | category | flops | bytes accessed | tf_op | source)
XLA Modules:
  0.0 685.1 jit_solution(11959686821084895500)
XLA Ops:
  9.1 2.4 bitcast_multiply_fusion
  18.5 13.5 %all-reduce = s32[32]{0:T(128)S(1)} all-reduce(s32[32]{0:T(128)S(1)} %bitcast_dynamic-update-slice_fusion.1), channel_id=2, replica_groups=mesh['site'=4,'blk'=16,'charge'=2] {'blk'}, use_global_device_ids=true, to_apply=%add | all-reduce | flops 32 | bytes 256
  32.1 11.6 %collective-permute-done = bf16[2,18,128,128]{3,2,1,0:T(8,128)(2,1)S(1)} collective-permute-done((bf16[2,18,128,128]{3,2,1,0:T(8,128)(2,1)}, bf16[2,18,128,128]{3,2,1,0:T(8,128)(2,1)S(1)}, u32[]{:S(2)}, u32[]{:S(2)}) %collective-permute-start) | collective-permute-done | bytes 1179680 | tf_op jit(solution)/shard_map/ppermute | solution.py:14
  47.0 77.2 %all-gather.3.cloned.1.call-done = bf16[32,128,2048]{2,1,0:T(8,128)(2,1)} async-done(((bf16[2,128,2048]{2,1,0:T(8,128)(2,1)}), bf16[32,128,2048]{2,1,0:T(8,128)(2,1)}) %all-gather.3.cloned.1.call-update) | async-done | bytes 16777232 | tf_op jit(solution)/shard_map/all_gather | solution.py:114
  124.2 26.1 %fusion.233 = bf16[2,2,128,2048]{3,1,2,0:T(2,128)(2,1)} fusion(bf16[32,128,2048]{2,1,0:T(8,128)(2,1)} %all-gather.3.cloned.1.call-done, s32[32]{0:T(128)S(1)} %all-reduce, s32[2,2]{1,0:T(2,128)S(1)} %broadcast_add_fusion), kind=kOutput, calls=%fused_computation.203 | convolution fusion | flops 68157568 | bytes 18874512 | tf_op jit(solution)/shard_map/kst,tam->ksam/dot_general | solution.py:71
  151.6 9.2 %collective-permute-start.2 = (bf16[2,18,128,128]{3,2,1,0:T(8,128)(2,1)S(1)}, bf16[2,18,128,128]{3,2,1,0:T(8,128)(2,1)}, u32[]{:S(2)}, u32[]{:S(2)}) collective-permute-start(bf16[2,18,128,128]{3,2,1,0:T(8,128)(2,1)S(1)} %get-tuple-element.589), channel_id=1, source_target_pairs={{0,32},{32,64},{64,96},{1,33},{33,65},{65,97},{2,34},{34,66},{66,9... | collective-permute-start | bytes 3538952 | tf_op jit(solution)/shard_map/ppermute | solution.py:14
  162.5 2.2 copy_multiply_fusion
  164.7 85.6 %collective-permute-done.2 = bf16[2,18,128,128]{3,2,1,0:T(8,128)(2,1)} collective-permute-done((bf16[2,18,128,128]{3,2,1,0:T(8,128)(2,1)S(1)}, bf16[2,18,128,128]{3,2,1,0:T(8,128)(2,1)}, u32[]{:S(2)}, u32[]{:S(2)}) %collective-permute-start.2) | collective-permute-done | bytes 1179680 | tf_op jit(solution)/shard_map/ppermute | solution.py:14
  250.4 2.7 select_select_fusion
  253.1 5.6 fusion.247
  258.6 7.1 %pad_maximum_fusion = bf16[2,3,128,2048]{3,1,2,0:T(4,128)(2,1)S(1)} fusion(bf16[2,1,128,2048]{3,1,2,0:T(2,128)(2,1)S(1)} %get-tuple-element.724, bf16[2,1,128,2048]{3,1,2,0:T(2,128)(2,1)S(1)} %copy_multiply_fusion, bf16[2,1,128,2048]{3,1,2,0:T(2,128)(2,1)S(1)} %get-tuple-element.723), kind=kLoop, calls=%fused_computation.198 | loop fusion | flops 9437184 | bytes 6291456 | tf_op jit(solution)/shard_map/stack | solution.py:119
  265.8 3.9 copy.100
  269.7 211.9 %while.113 = (s32[]{:T(128)}, f32[2,128,2048]{2,1,0:T(8,128)}, bf16[2,18,128,128]{3,2,1,0:T(8,128)(2,1)S(1)}, bf16[2,18,128,128]{3,2,1,0:T(8,128)(2,1)}, bf16[2,...) while((s32[]{:T(128)}, f32[2,128,2048]{2,1,0:T(8,128)}, ...), condition=%wide.region_27.28_spmd, body=%wide.region_24.27_spmd.sunk | while | flops 143654912 | bytes 23926256 | solution.py:125
  269.7 2.4 dynamic-slice_bitcast_fusion.5
  272.1 2.7 dynamic-slice_bitcast_fusion.6
  274.8 99.1 %while.114 = (s32[]{:T(128)}, f32[128,2048]{1,0:T(8,128)S(1)}, bf16[18,16,16]{1,2,0:T(8,128)(2,1)}, bf16[18,128,128]{2,1,0:T(8,128)(2,1)}, s32[18]{0:T(128)S(1)}...) while((s32[]{:T(128)}, f32[128,2048]{1,0:T(8,128)S(1)}, ...), condition=%wide.region_26.26_spmd.clone, body=%wide.region_25.25_spmd.clone.sunk | while | flops 143654912 | bytes 6886593 | solution.py:54
  375.6 2.4 dynamic-slice_bitcast_fusion.5
  378.0 2.7 dynamic-slice_bitcast_fusion.6
  380.7 99.1 %while.114 = (s32[]{:T(128)}, f32[128,2048]{1,0:T(8,128)S(1)}, bf16[18,16,16]{1,2,0:T(8,128)(2,1)}, bf16[18,128,128]{2,1,0:T(8,128)(2,1)}, s32[18]{0:T(128)S(1)}...) while((s32[]{:T(128)}, f32[128,2048]{1,0:T(8,128)S(1)}, ...), condition=%wide.region_26.26_spmd.clone, body=%wide.region_25.25_spmd.clone.sunk | while | flops 143654912 | bytes 6886593 | solution.py:54
  481.5 3.8 fusion.238
  485.3 68.7 %all-reduce.1 = (f32[]{:T(128)}, f32[]{:T(128)}) all-reduce(f32[]{:T(128)} %get-tuple-element.594, f32[]{:T(128)} %get-tuple-element.593), channel_id=1, replica_groups=mesh['site'=4,'blk'=16,'charge'=2] {'blk','charge'}, use_global_device_ids=true, to_apply=%region_29.30 | all-reduce | flops 2 | bytes 16 | tf_op jit(solution)/shard_map/psum | solution.py:132
  555.4 3.3 multiply_reduce_fusion
  558.7 48.6 %conditional.7 = (bf16[1,2,18,128,128]{4,3,2,1,0:T(8,128)(2,1)}) conditional(s32[]{:T(128)} %convert_element_type.194, (bf16[2,18,128,128]{3,2,1,0:T(8,128)(2,1)S(1)}) %tuple.289, (bf16[2,2,4,128,128]{3,4,2,1,0:T(8,128)(2,1)}, bf16[2,18,18,4,4]{1,2,4,3,0:T(8,128)(2,1)}, bf16[2,18,128,128]{3,2,1,0:T(8,128)(2,1)S(1)}) %tuple.290), branch_computations={%region_18.19_spmd, %region_19.24_spmd} | conditional | flops 1553006592 | bytes 31303274 | solution.py:100
  558.7 1.9 slice_bitcast_fusion.12
  562.5 21.7 %while.109 = (s32[]{:T(128)}, bf16[2,18,128,128]{2,3,1,0:T(8,128)(2,1)S(1)}, bf16[2,4,128,128]{2,3,1,0:T(8,128)(2,1)}, bf16[2,18,128,128]{3,2,1,0:T(8,128)(2,1)S(1)}, bf16[18,18,4,4]{0,1,3,2:T(8,128)(2,1)}, /*index=5*/s32[]{:T(128)}) while((s32[]{:T(128)}, bf16[2,18,128,128]{2,3,1,0:T(8,128)(2,1)S(1)}, bf16[2,4,128,128]{2,3,1,0:T(8,128)(2,1)}, ...), condition=%wide.region_21.21_spmd, body=%wide.region_20.20_spmd.sunk | while | flops 776503296 | bytes 12768005 | solution.py:35
  564.4 7.2 %fusion.333 = bf16[18,4,128,128]{2,0,1,3:T(8,128)(2,1)S(1)} fusion(bf16[18,4,128,128,1]{2,3,0,1,4:T(8,128)(2,1)S(1)} %convert_bitcast_fusion.16, bf16[18,18,4,4]{0,1,3,2:T(8,128)(2,1)S(1)} %copy-done.20), kind=kOutput, calls=%fused_computation.133.clone.1 | convolution fusion | flops 171048960 | bytes 4728960 | tf_op jit(solution)/shard_map/cond/branch_1_fun/while/body/eval_jaxpr/wvts,wsac->vtac/dot_general | solution.py:28
  575.2 7.2 %fusion.333 = bf16[18,4,128,128]{2,0,1,3:T(8,128)(2,1)S(1)} fusion(bf16[18,4,128,128,1]{2,3,0,1,4:T(8,128)(2,1)S(1)} %convert_bitcast_fusion.16, bf16[18,18,4,4]{0,1,3,2:T(8,128)(2,1)S(1)} %copy-done.20), kind=kOutput, calls=%fused_computation.133.clone.1 | convolution fusion | flops 171048960 | bytes 4728960 | tf_op jit(solution)/shard_map/cond/branch_1_fun/while/body/eval_jaxpr/wvts,wsac->vtac/dot_general | solution.py:28
  584.4 21.3 %while.110 = (s32[]{:T(128)}, bf16[2,18,128,128]{2,3,1,0:T(8,128)(2,1)S(1)}, bf16[2,4,128,128]{2,3,1,0:T(8,128)(2,1)}, bf16[2,18,128,128]{2,3,1,0:T(8,128)(2,1)S...) while((s32[]{:T(128)}, bf16[2,18,128,128]{2,3,1,0:T(8,128)(2,1)S(1)}, ...), condition=%wide.region_23.23_spmd, body=%wide.region_22.22_spmd.sunk | while | flops 776503296 | bytes 12726505 | solution.py:35
  586.1 7.2 %fusion.341 = bf16[18,4,128,128]{2,0,1,3:T(8,128)(2,1)S(1)} fusion(bf16[18,4,128,128,1]{2,3,0,1,4:T(8,128)(2,1)S(1)} %convert_bitcast_fusion.17, bf16[18,18,4,4]{0,1,3,2:T(8,128)(2,1)S(1)} %get-tuple-element.1151), kind=kOutput, calls=%fused_computation.153.clone.1 | convolution fusion | flops 171048960 | bytes 4728960 | tf_op jit(solution)/shard_map/cond/branch_1_fun/while/body/eval_jaxpr/wvts,wsac->vtac/dot_general | solution.py:28
  596.8 7.2 %fusion.341 = bf16[18,4,128,128]{2,0,1,3:T(8,128)(2,1)S(1)} fusion(bf16[18,4,128,128,1]{2,3,0,1,4:T(8,128)(2,1)S(1)} %convert_bitcast_fusion.17, bf16[18,18,4,4]{0,1,3,2:T(8,128)(2,1)S(1)} %get-tuple-element.1151), kind=kOutput, calls=%fused_computation.153.clone.1 | convolution fusion | flops 171048960 | bytes 4728960 | tf_op jit(solution)/shard_map/cond/branch_1_fun/while/body/eval_jaxpr/wvts,wsac->vtac/dot_general | solution.py:28
  607.4 65.9 %psum.23 = f32[]{:T(128)} all-reduce(f32[]{:T(128)} %multiply_reduce_fusion), channel_id=1, replica_groups=mesh['site'=4,'blk'=16,'charge'=2] {'blk','charge'}, use_global_device_ids=true, to_apply=%region_33.34 | all-reduce | flops 1 | bytes 8 | tf_op jit(solution)/shard_map/psum | solution.py:137
  674.0 3.3 fusion.240
  (273 shorter events, 183.8 us)
Async XLA Ops:
  7.2 4.4 copy-start.18
  7.2 5.4 copy-start.17
  7.2 117.0 %all-gather.3.cloned.1.call-start = ((), (), s32[]{:S(2)}) async-start(), calls=%async_computation | async-start | bytes 17825792 | tf_op jit(solution)/shard_map/all_gather | solution.py:114
  8.6 0.5 copy-start.21
  9.1 4.5 copy-start.2
  13.6 2.3 copy-start.26
  13.6 3.4 copy-start.28
  13.6 18.4 %copy-start.25 = (s32[2]{0:T(128)S(1)}, s32[2]{0:T(128)}, u32[]{:S(2)}) copy-start(s32[2]{0:T(128)} %constant.168.clone) | copy-start | bytes 28
  14.7 29.0 %collective-permute-start = (bf16[2,18,128,128]{3,2,1,0:T(8,128)(2,1)}, bf16[2,18,128,128]{3,2,1,0:T(8,128)(2,1)S(1)}, u32[]{:S(2)}, u32[]{:S(2)}) collective-permute-start(bf16[2,18,128,128]{3,2,1,0:T(8,128)(2,1)} %get-tuple-element.585), channel_id=1, source_target_pairs={{0,32},{32,64},{64,96},{1,33},{33,65},{65,97},{2,34},{34,66},{66,9... | collective-permute-start | bytes 3538952 | tf_op jit(solution)/shard_map/ppermute | solution.py:14
  16.0 16.0 %collective-permute-start.3 = (s32[2]{0:T(128)S(1)}, s32[2]{0:T(128)S(1)}, u32[]{:S(2)}, u32[]{:S(2)}) collective-permute-start(s32[2]{0:T(128)S(1)} %bitcast.620), channel_id=1, source_target_pairs={{0,1},{1,0},{2,3},{3,2},{4,5},{5,4},{6,7},{7,6},{8,9},{9,8},{10,11... | collective-permute-start | bytes 32 | tf_op jit(solution)/shard_map/ppermute | solution.py:18
  43.7 1.8 copy-start.8
  45.6 105.5 %collective-permute-start.1 = (bf16[2,18,128,128]{3,2,1,0:T(8,128)(2,1)S(1)}, bf16[2,18,128,128]{3,2,1,0:T(8,128)(2,1)}, u32[]{:S(2)}, u32[]{:S(2)}) collective-permute-start(bf16[2,18,128,128]{3,2,1,0:T(8,128)(2,1)S(1)} %get-tuple-element.587), channel_id=1, source_target_pairs={{0,32},{32,64},{64,96},{1,33},{33,65},{65,97},{2,34},{34,66},{66,9... | collective-permute-start | bytes 3538952 | tf_op jit(solution)/shard_map/ppermute | solution.py:14
  150.3 102.7 %collective-permute-start.4 = (bf16[2,2,128,2048]{3,1,2,0:T(2,128)(2,1)}, bf16[2,2,128,2048]{3,1,2,0:T(2,128)(2,1)}, u32[]{:S(2)}, u32[]{:S(2)}) collective-permute-start(bf16[2,2,128,2048]{3,1,2,0:T(2,128)(2,1)} %fusion.233), channel_id=1, source_target_pairs={{0,1},{1,0},{2,3},{3,2},{4,5},{5,4},{6,7},{7,6},{8,9},{9,8},{10,11... | collective-permute-start | bytes 6291464 | tf_op jit(solution)/shard_map/ppermute | solution.py:18
  151.2 11.3 %copy-start = (bf16[1,2,128,2048]{3,2,1,0:T(8,128)(2,1)S(1)}, bf16[1,2,128,2048]{3,2,1,0:T(8,128)(2,1)}, u32[]{:S(2)}) copy-start(bf16[1,2,128,2048]{3,2,1,0:T(8,128)(2,1)} %param.39) | copy-start | bytes 3145732
  151.2 11.3 %copy-start.22 = (bf16[2,128]{1,0:T(2,128)(2,1)S(1)}, bf16[2,128]{1,0:T(2,128)(2,1)}, u32[]{:S(2)}) copy-start(bf16[2,128]{1,0:T(2,128)(2,1)} %copy-done.21) | copy-start | bytes 1540
  151.6 98.7 %collective-permute-start.2 = (bf16[2,18,128,128]{3,2,1,0:T(8,128)(2,1)S(1)}, bf16[2,18,128,128]{3,2,1,0:T(8,128)(2,1)}, u32[]{:S(2)}, u32[]{:S(2)}) collective-permute-start(bf16[2,18,128,128]{3,2,1,0:T(8,128)(2,1)S(1)} %get-tuple-element.589), channel_id=1, source_target_pairs={{0,32},{32,64},{64,96},{1,33},{33,65},{65,97},{2,34},{34,66},{66,9... | collective-permute-start | bytes 3538952 | tf_op jit(solution)/shard_map/ppermute | solution.py:14
  162.5 87.9 %copy-start.9 = (bf16[2,18,128,128]{3,2,1,0:T(8,128)(2,1)S(1)}, bf16[2,18,128,128]{3,2,1,0:T(8,128)(2,1)}, u32[]{:S(2)}) copy-start(bf16[2,18,128,128]{3,2,1,0:T(8,128)(2,1)} %copy-done.8) | copy-start | bytes 3538948
  265.8 3.9 copy-start.27
  269.7 211.9 %copy-start.23 = (f32[2,128]{1,0:T(2,128)S(1)}, f32[2,128]{1,0:T(2,128)}, u32[]{:S(2)}) copy-start(f32[2,128]{1,0:T(2,128)} %get-tuple-element.727) | copy-start | bytes 3076
  269.7 211.9 %copy-start.24 = (f32[1,2]{1,0:T(1,128)S(1)}, f32[1,2]{1,0:T(1,128)}, u32[]{:S(2)}) copy-start(f32[1,2]{1,0:T(1,128)} %param.45) | copy-start | bytes 28
  269.7 5.2 copy-start.4
  374.0 1.6 copy-start.5
  375.6 5.1 copy-start.4
  479.9 1.6 copy-start.5
  481.5 73.8 %copy-start.1 = (bf16[1,2,128,2048]{3,2,1,0:T(8,128)(2,1)S(1)}, bf16[1,2,128,2048]{3,2,1,0:T(8,128)(2,1)}, u32[]{:S(2)}) copy-start(bf16[1,2,128,2048]{3,2,1,0:T(8,128)(2,1)} %param.39) | copy-start | bytes 3145732
  481.5 73.8 %copy-start.3 = (bf16[2,18,128,128]{3,2,1,0:T(8,128)(2,1)S(1)}, bf16[2,18,128,128]{3,2,1,0:T(8,128)(2,1)}, u32[]{:S(2)}) copy-start(bf16[2,18,128,128]{3,2,1,0:T(8,128)(2,1)} %get-tuple-element.726) | copy-start | bytes 3538948
  562.7 1.7 copy-start.20
  564.4 7.2 %copy-start.14 = (bf16[2,4,128,128]{2,3,1,0:T(8,128)(2,1)S(1)}, bf16[2,4,128,128]{2,3,1,0:T(8,128)(2,1)}, u32[]{:S(2)}) copy-start(bf16[2,4,128,128]{2,3,1,0:T(8,128)(2,1)} %get-tuple-element.1131) | copy-start | bytes 786436 | tf_op jit(solution)/shard_map/cond/branch_1_fun/while
  573.4 1.7 copy-start.20
  575.2 7.2 %copy-start.14 = (bf16[2,4,128,128]{2,3,1,0:T(8,128)(2,1)S(1)}, bf16[2,4,128,128]{2,3,1,0:T(8,128)(2,1)}, u32[]{:S(2)}) copy-start(bf16[2,4,128,128]{2,3,1,0:T(8,128)(2,1)} %get-tuple-element.1131) | copy-start | bytes 786436 | tf_op jit(solution)/shard_map/cond/branch_1_fun/while
  586.1 7.2 %copy-start.11 = (bf16[2,4,128,128]{2,3,1,0:T(8,128)(2,1)S(1)}, bf16[2,4,128,128]{2,3,1,0:T(8,128)(2,1)}, u32[]{:S(2)}) copy-start(bf16[2,4,128,128]{2,3,1,0:T(8,128)(2,1)} %get-tuple-element.1149) | copy-start | bytes 786436 | tf_op jit(solution)/shard_map/cond/branch_1_fun/while
  596.7 7.2 %copy-start.11 = (bf16[2,4,128,128]{2,3,1,0:T(8,128)(2,1)S(1)}, bf16[2,4,128,128]{2,3,1,0:T(8,128)(2,1)}, u32[]{:S(2)}) copy-start(bf16[2,4,128,128]{2,3,1,0:T(8,128)(2,1)} %get-tuple-element.1149) | copy-start | bytes 786436 | tf_op jit(solution)/shard_map/cond/branch_1_fun/while
Sparse Core Ops, SparseCore 0:
  11.7 112.4 all-gather.2
where the time goes:
time: 698 us; the launch traced here: 685 us
  waiting for transfers between devices  174 us (25%)
  matrix products  161 us (23%)
  blocking collectives  148 us (21%)
  local copies, waits for them, and re-layouts  62.4 us (9%)
  other arithmetic  56 us (8%)
  loops' own time  52.4 us (8%)
  between operations  17.4 us (2%)
  starting transfers between devices  13.8 us (2%)
    ppermute x3, waiting for transfers between devices, from_behind(): return lax.ppermute(block, axis, route)  97.3 us
    all_gather x1, waiting for transfers between devices, on_device(): lax.all_gather(theta_m, 'blk', axis=0, tiled=True)  77.2 us
    psum x1, blocking collectives, on_device(): lax.psum((jnp.sum(theta_f * product), jnp.sum(theta_f * theta_f)), ('blk'...  68.7 us
    psum x1, blocking collectives, on_device(): residual_sq = lax.psum(jnp.sum(residual * residual), ('blk', 'charge'))  65.9 us
    another operation x2, loops' own time, block_product(): lax.scan(segment, start_sum, (env_block, right_blocks, ops, charges))[0]  51.2 us
    dot_general x36, matrix products, segment(): jnp.dot(left_block, source_tile, preferred_element_type=jnp.float32)  48.7 us
    dot_general x36, matrix products, segment(): jnp.einsum('asc,st->atc', applied, bond_op, preferred_element_type=jnp.fl...  43.4 us
    dot_general x4, matrix products, one_block(): jnp.einsum('wvts,wsac->vtac', site_op, left_part, preferred_element_type=...  28.8 us
  transfers between devices with their start and end apart: 6, of which 3 were waited for; matrix products, arithmetic and copies ran while one was open for 6% of the time, Pallas kernels for 0%

commit v1 on v0

--- a/solution.py
+++ b/solution.py
@@ -130,7 +130,7 @@
     )
     entries_count = NS * BS * M
     correlation, norm_theta = lax.psum(
-        (jnp.sum(theta_f * product), jnp.sum(theta_f * theta_f)), ("blk", "charge")
+        lax.psum((jnp.sum(theta_f * product), jnp.sum(theta_f * theta_f)), "charge"), "blk"
     )
     rayleigh = correlation / norm_theta
     residual = product - rayleigh * theta_f

time: 698 us -> 664 us (0.951)
  blocking collectives: 148 us -> 126 us
  loops' own time: 52.4 us -> 43.2 us
    psum x1 -> x2, blocking collectives: 68.7 us -> 42.7 us  [the longest x1 36.8 us: on_device(): lax.psum(lax.psum((jnp.sum(theta_f * product), jnp.sum(theta_f * theta_f)...]
    another operation x2, loops' own time: 51.2 us -> 42 us  [block_product(): lax.scan(segment, start_sum, (env_block, right_blocks, ops, charges))[0]]
where the time goes in v1:
time: 664 us; the launch traced here: 651 us
  waiting for transfers between devices  174 us (26%)
  matrix products  161 us (24%)
  blocking collectives  126 us (19%)
  local copies, waits for them, and re-layouts  59.4 us (9%)
  other arithmetic  55.9 us (8%)
  loops' own time  43.2 us (7%)
  between operations  17.5 us (3%)
  starting transfers between devices  13.8 us (2%)
    ppermute x3, waiting for transfers between devices, from_behind(): return lax.ppermute(block, axis, route)  97.2 us
    all_gather x1, waiting for transfers between devices, on_device(): lax.all_gather(theta_m, 'blk', axis=0, tiled=True)  77.2 us
    psum x1, blocking collectives, on_device(): residual_sq = lax.psum(jnp.sum(residual * residual), ('blk', 'charge'))  70 us
    dot_general x36, matrix products, segment(): jnp.dot(left_block, source_tile, preferred_element_type=jnp.float32)  48.7 us
    dot_general x36, matrix products, segment(): jnp.einsum('asc,st->atc', applied, bond_op, preferred_element_type=jnp.fl...  43.4 us
    another operation x2, loops' own time, block_product(): lax.scan(segment, start_sum, (env_block, right_blocks, ops, charges))[0]  42 us
    psum x1, blocking collectives, on_device(): lax.psum(lax.psum((jnp.sum(theta_f * product), jnp.sum(theta_f * theta_f)...  36.8 us
    dot_general x4, matrix products, one_block(): jnp.einsum('wvts,wsac->vtac', site_op, left_part, preferred_element_type=...  28.8 us
  transfers between devices with their start and end apart: 6, of which 3 were waited for; matrix products, arithmetic and copies ran while one was open for 6% of the time, Pallas kernels for 0%

profile of v1, /device:TPU:97, one launch (start us, length us, event | category | flops | bytes accessed | tf_op | source)
XLA Modules:
  0.0 651.1 jit_solution(12746286979228795503)
XLA Ops:
  9.1 2.4 bitcast_multiply_fusion
  18.5 13.5 %all-reduce = s32[32]{0:T(128)S(1)} all-reduce(s32[32]{0:T(128)S(1)} %bitcast_dynamic-update-slice_fusion.1), channel_id=2, replica_groups=mesh['site'=4,'blk'=16,'charge'=2] {'blk'}, use_global_device_ids=true, to_apply=%add | all-reduce | flops 32 | bytes 256
  32.1 11.6 %collective-permute-done = bf16[2,18,128,128]{3,2,1,0:T(8,128)(2,1)S(1)} collective-permute-done((bf16[2,18,128,128]{3,2,1,0:T(8,128)(2,1)}, bf16[2,18,128,128]{3,2,1,0:T(8,128)(2,1)S(1)}, u32[]{:S(2)}, u32[]{:S(2)}) %collective-permute-start) | collective-permute-done | bytes 1179680 | tf_op jit(solution)/shard_map/ppermute | solution.py:14
  47.0 77.2 %all-gather.3.cloned.1.call-done = bf16[32,128,2048]{2,1,0:T(8,128)(2,1)} async-done(((bf16[2,128,2048]{2,1,0:T(8,128)(2,1)}), bf16[32,128,2048]{2,1,0:T(8,128)(2,1)}) %all-gather.3.cloned.1.call-update) | async-done | bytes 16777232 | tf_op jit(solution)/shard_map/all_gather | solution.py:114
  124.2 26.1 %fusion.233 = bf16[2,2,128,2048]{3,1,2,0:T(2,128)(2,1)} fusion(bf16[32,128,2048]{2,1,0:T(8,128)(2,1)} %all-gather.3.cloned.1.call-done, s32[32]{0:T(128)S(1)} %all-reduce, s32[2,2]{1,0:T(2,128)S(1)} %broadcast_add_fusion), kind=kOutput, calls=%fused_computation.203 | convolution fusion | flops 68157568 | bytes 18874512 | tf_op jit(solution)/shard_map/kst,tam->ksam/dot_general | solution.py:71
  151.6 9.2 %collective-permute-start.2 = (bf16[2,18,128,128]{3,2,1,0:T(8,128)(2,1)S(1)}, bf16[2,18,128,128]{3,2,1,0:T(8,128)(2,1)}, u32[]{:S(2)}, u32[]{:S(2)}) collective-permute-start(bf16[2,18,128,128]{3,2,1,0:T(8,128)(2,1)S(1)} %get-tuple-element.589), channel_id=1, source_target_pairs={{0,32},{32,64},{64,96},{1,33},{33,65},{65,97},{2,34},{34,66},{66,9... | collective-permute-start | bytes 3538952 | tf_op jit(solution)/shard_map/ppermute | solution.py:14
  162.5 2.2 copy_multiply_fusion
  164.8 85.6 %collective-permute-done.2 = bf16[2,18,128,128]{3,2,1,0:T(8,128)(2,1)} collective-permute-done((bf16[2,18,128,128]{3,2,1,0:T(8,128)(2,1)S(1)}, bf16[2,18,128,128]{3,2,1,0:T(8,128)(2,1)}, u32[]{:S(2)}, u32[]{:S(2)}) %collective-permute-start.2) | collective-permute-done | bytes 1179680 | tf_op jit(solution)/shard_map/ppermute | solution.py:14
  250.4 2.7 select_select_fusion
  253.1 5.6 fusion.247
  258.7 7.1 %pad_maximum_fusion = bf16[2,3,128,2048]{3,1,2,0:T(4,128)(2,1)S(1)} fusion(bf16[2,1,128,2048]{3,1,2,0:T(2,128)(2,1)S(1)} %get-tuple-element.726, bf16[2,1,128,2048]{3,1,2,0:T(2,128)(2,1)S(1)} %copy_multiply_fusion, bf16[2,1,128,2048]{3,1,2,0:T(2,128)(2,1)S(1)} %get-tuple-element.725), kind=kLoop, calls=%fused_computation.198 | loop fusion | flops 9437184 | bytes 6291456 | tf_op jit(solution)/shard_map/stack | solution.py:119
  265.8 3.9 copy.100
  269.7 199.8 %while.113 = (s32[]{:T(128)}, f32[2,128,2048]{2,1,0:T(8,128)}, bf16[2,18,128,128]{3,2,1,0:T(8,128)(2,1)S(1)}, bf16[2,18,128,128]{3,2,1,0:T(8,128)(2,1)}, bf16[2,...) while((s32[]{:T(128)}, f32[2,128,2048]{2,1,0:T(8,128)}, ...), condition=%wide.region_27.28_spmd, body=%wide.region_24.27_spmd.sunk | while | flops 143654912 | bytes 23926256 | solution.py:125
  269.7 2.4 dynamic-slice_bitcast_fusion.5
  272.1 2.8 dynamic-slice_bitcast_fusion.6
  274.9 93.1 %while.114 = (s32[]{:T(128)}, f32[128,2048]{1,0:T(8,128)S(1)}, bf16[18,16,16]{1,2,0:T(8,128)(2,1)}, bf16[18,128,128]{2,1,0:T(8,128)(2,1)}, s32[18]{0:T(128)S(1)}...) while((s32[]{:T(128)}, f32[128,2048]{1,0:T(8,128)S(1)}, ...), condition=%wide.region_26.26_spmd.clone, body=%wide.region_25.25_spmd.clone.sunk | while | flops 143654912 | bytes 6886593 | solution.py:54
  369.6 2.4 dynamic-slice_bitcast_fusion.5
  372.0 2.8 dynamic-slice_bitcast_fusion.6
  374.8 93.1 %while.114 = (s32[]{:T(128)}, f32[128,2048]{1,0:T(8,128)S(1)}, bf16[18,16,16]{1,2,0:T(8,128)(2,1)}, bf16[18,128,128]{2,1,0:T(8,128)(2,1)}, s32[18]{0:T(128)S(1)}...) while((s32[]{:T(128)}, f32[128,2048]{1,0:T(8,128)S(1)}, ...), condition=%wide.region_26.26_spmd.clone, body=%wide.region_25.25_spmd.clone.sunk | while | flops 143654912 | bytes 6886593 | solution.py:54
  469.5 3.8 fusion.238
  473.3 6.0 all-reduce.2
  479.3 36.8 %all-reduce.1 = (f32[]{:T(128)}, f32[]{:T(128)}) all-reduce(f32[]{:T(128)} %get-tuple-element.705, f32[]{:T(128)} %get-tuple-element.706), channel_id=1, replica_groups=mesh['site'=4,'blk'=16,'charge'=2] {'blk'}, use_global_device_ids=true, to_apply=%region_30.31 | all-reduce | flops 2 | bytes 16 | tf_op jit(solution)/shard_map/psum | solution.py:132
  517.4 3.2 multiply_reduce_fusion
  520.6 48.6 %conditional.7 = (bf16[1,2,18,128,128]{4,3,2,1,0:T(8,128)(2,1)}) conditional(s32[]{:T(128)} %convert_element_type.194, (bf16[2,18,128,128]{3,2,1,0:T(8,128)(2,1)S(1)}) %tuple.289, (bf16[2,2,4,128,128]{3,4,2,1,0:T(8,128)(2,1)}, bf16[2,18,18,4,4]{1,2,4,3,0:T(8,128)(2,1)}, bf16[2,18,128,128]{3,2,1,0:T(8,128)(2,1)S(1)}) %tuple.290), branch_computations={%region_18.19_spmd, %region_19.24_spmd} | conditional | flops 1553006592 | bytes 31303274 | solution.py:100
  524.4 21.7 %while.109 = (s32[]{:T(128)}, bf16[2,18,128,128]{2,3,1,0:T(8,128)(2,1)S(1)}, bf16[2,4,128,128]{2,3,1,0:T(8,128)(2,1)}, bf16[2,18,128,128]{3,2,1,0:T(8,128)(2,1)S(1)}, bf16[18,18,4,4]{0,1,3,2:T(8,128)(2,1)}, /*index=5*/s32[]{:T(128)}) while((s32[]{:T(128)}, bf16[2,18,128,128]{2,3,1,0:T(8,128)(2,1)S(1)}, bf16[2,4,128,128]{2,3,1,0:T(8,128)(2,1)}, ...), condition=%wide.region_21.21_spmd, body=%wide.region_20.20_spmd.sunk | while | flops 776503296 | bytes 12768005 | solution.py:35
  526.3 7.2 %fusion.333 = bf16[18,4,128,128]{2,0,1,3:T(8,128)(2,1)S(1)} fusion(bf16[18,4,128,128,1]{2,3,0,1,4:T(8,128)(2,1)S(1)} %convert_bitcast_fusion.16, bf16[18,18,4,4]{0,1,3,2:T(8,128)(2,1)S(1)} %copy-done.20), kind=kOutput, calls=%fused_computation.133.clone.1 | convolution fusion | flops 171048960 | bytes 4728960 | tf_op jit(solution)/shard_map/cond/branch_1_fun/while/body/eval_jaxpr/wvts,wsac->vtac/dot_general | solution.py:28
  537.1 7.2 %fusion.333 = bf16[18,4,128,128]{2,0,1,3:T(8,128)(2,1)S(1)} fusion(bf16[18,4,128,128,1]{2,3,0,1,4:T(8,128)(2,1)S(1)} %convert_bitcast_fusion.16, bf16[18,18,4,4]{0,1,3,2:T(8,128)(2,1)S(1)} %copy-done.20), kind=kOutput, calls=%fused_computation.133.clone.1 | convolution fusion | flops 171048960 | bytes 4728960 | tf_op jit(solution)/shard_map/cond/branch_1_fun/while/body/eval_jaxpr/wvts,wsac->vtac/dot_general | solution.py:28
  546.3 21.3 %while.110 = (s32[]{:T(128)}, bf16[2,18,128,128]{2,3,1,0:T(8,128)(2,1)S(1)}, bf16[2,4,128,128]{2,3,1,0:T(8,128)(2,1)}, bf16[2,18,128,128]{2,3,1,0:T(8,128)(2,1)S...) while((s32[]{:T(128)}, bf16[2,18,128,128]{2,3,1,0:T(8,128)(2,1)S(1)}, ...), condition=%wide.region_23.23_spmd, body=%wide.region_22.22_spmd.sunk | while | flops 776503296 | bytes 12726505 | solution.py:35
  548.0 7.2 %fusion.341 = bf16[18,4,128,128]{2,0,1,3:T(8,128)(2,1)S(1)} fusion(bf16[18,4,128,128,1]{2,3,0,1,4:T(8,128)(2,1)S(1)} %convert_bitcast_fusion.17, bf16[18,18,4,4]{0,1,3,2:T(8,128)(2,1)S(1)} %get-tuple-element.1153), kind=kOutput, calls=%fused_computation.153.clone.1 | convolution fusion | flops 171048960 | bytes 4728960 | tf_op jit(solution)/shard_map/cond/branch_1_fun/while/body/eval_jaxpr/wvts,wsac->vtac/dot_general | solution.py:28
  558.6 7.2 %fusion.341 = bf16[18,4,128,128]{2,0,1,3:T(8,128)(2,1)S(1)} fusion(bf16[18,4,128,128,1]{2,3,0,1,4:T(8,128)(2,1)S(1)} %convert_bitcast_fusion.17, bf16[18,18,4,4]{0,1,3,2:T(8,128)(2,1)S(1)} %get-tuple-element.1153), kind=kOutput, calls=%fused_computation.153.clone.1 | convolution fusion | flops 171048960 | bytes 4728960 | tf_op jit(solution)/shard_map/cond/branch_1_fun/while/body/eval_jaxpr/wvts,wsac->vtac/dot_general | solution.py:28
  569.3 70.0 %psum.39 = f32[]{:T(128)} all-reduce(f32[]{:T(128)} %multiply_reduce_fusion), channel_id=1, replica_groups=mesh['site'=4,'blk'=16,'charge'=2] {'blk','charge'}, use_global_device_ids=true, to_apply=%region_35.36 | all-reduce | flops 1 | bytes 8 | tf_op jit(solution)/shard_map/psum | solution.py:137
  640.0 3.3 fusion.240
  (274 shorter events, 182.7 us)
Async XLA Ops:
  7.2 4.4 copy-start.18
  7.2 5.4 copy-start.17
  7.2 117.0 %all-gather.3.cloned.1.call-start = ((), (), s32[]{:S(2)}) async-start(), calls=%async_computation | async-start | bytes 17825792 | tf_op jit(solution)/shard_map/all_gather | solution.py:114
  8.6 0.5 copy-start.21
  9.1 4.5 copy-start.2
  13.6 2.3 copy-start.26
  13.6 3.4 copy-start.28
  13.6 18.4 %copy-start.25 = (s32[2]{0:T(128)S(1)}, s32[2]{0:T(128)}, u32[]{:S(2)}) copy-start(s32[2]{0:T(128)} %constant.168.clone) | copy-start | bytes 28
  14.7 29.0 %collective-permute-start = (bf16[2,18,128,128]{3,2,1,0:T(8,128)(2,1)}, bf16[2,18,128,128]{3,2,1,0:T(8,128)(2,1)S(1)}, u32[]{:S(2)}, u32[]{:S(2)}) collective-permute-start(bf16[2,18,128,128]{3,2,1,0:T(8,128)(2,1)} %get-tuple-element.585), channel_id=1, source_target_pairs={{0,32},{32,64},{64,96},{1,33},{33,65},{65,97},{2,34},{34,66},{66,9... | collective-permute-start | bytes 3538952 | tf_op jit(solution)/shard_map/ppermute | solution.py:14
  16.0 16.0 %collective-permute-start.3 = (s32[2]{0:T(128)S(1)}, s32[2]{0:T(128)S(1)}, u32[]{:S(2)}, u32[]{:S(2)}) collective-permute-start(s32[2]{0:T(128)S(1)} %bitcast.620), channel_id=1, source_target_pairs={{0,1},{1,0},{2,3},{3,2},{4,5},{5,4},{6,7},{7,6},{8,9},{9,8},{10,11... | collective-permute-start | bytes 32 | tf_op jit(solution)/shard_map/ppermute | solution.py:18
  43.7 1.8 copy-start.8
  45.6 105.5 %collective-permute-start.1 = (bf16[2,18,128,128]{3,2,1,0:T(8,128)(2,1)S(1)}, bf16[2,18,128,128]{3,2,1,0:T(8,128)(2,1)}, u32[]{:S(2)}, u32[]{:S(2)}) collective-permute-start(bf16[2,18,128,128]{3,2,1,0:T(8,128)(2,1)S(1)} %get-tuple-element.587), channel_id=1, source_target_pairs={{0,32},{32,64},{64,96},{1,33},{33,65},{65,97},{2,34},{34,66},{66,9... | collective-permute-start | bytes 3538952 | tf_op jit(solution)/shard_map/ppermute | solution.py:14
  150.3 102.8 %collective-permute-start.4 = (bf16[2,2,128,2048]{3,1,2,0:T(2,128)(2,1)}, bf16[2,2,128,2048]{3,1,2,0:T(2,128)(2,1)}, u32[]{:S(2)}, u32[]{:S(2)}) collective-permute-start(bf16[2,2,128,2048]{3,1,2,0:T(2,128)(2,1)} %fusion.233), channel_id=1, source_target_pairs={{0,1},{1,0},{2,3},{3,2},{4,5},{5,4},{6,7},{7,6},{8,9},{9,8},{10,11... | collective-permute-start | bytes 6291464 | tf_op jit(solution)/shard_map/ppermute | solution.py:18
  151.2 11.4 %copy-start = (bf16[1,2,128,2048]{3,2,1,0:T(8,128)(2,1)S(1)}, bf16[1,2,128,2048]{3,2,1,0:T(8,128)(2,1)}, u32[]{:S(2)}) copy-start(bf16[1,2,128,2048]{3,2,1,0:T(8,128)(2,1)} %param.39) | copy-start | bytes 3145732
  151.2 11.4 %copy-start.22 = (bf16[2,128]{1,0:T(2,128)(2,1)S(1)}, bf16[2,128]{1,0:T(2,128)(2,1)}, u32[]{:S(2)}) copy-start(bf16[2,128]{1,0:T(2,128)(2,1)} %copy-done.21) | copy-start | bytes 1540
  151.6 98.8 %collective-permute-start.2 = (bf16[2,18,128,128]{3,2,1,0:T(8,128)(2,1)S(1)}, bf16[2,18,128,128]{3,2,1,0:T(8,128)(2,1)}, u32[]{:S(2)}, u32[]{:S(2)}) collective-permute-start(bf16[2,18,128,128]{3,2,1,0:T(8,128)(2,1)S(1)} %get-tuple-element.589), channel_id=1, source_target_pairs={{0,32},{32,64},{64,96},{1,33},{33,65},{65,97},{2,34},{34,66},{66,9... | collective-permute-start | bytes 3538952 | tf_op jit(solution)/shard_map/ppermute | solution.py:14
  162.5 87.9 %copy-start.9 = (bf16[2,18,128,128]{3,2,1,0:T(8,128)(2,1)S(1)}, bf16[2,18,128,128]{3,2,1,0:T(8,128)(2,1)}, u32[]{:S(2)}) copy-start(bf16[2,18,128,128]{3,2,1,0:T(8,128)(2,1)} %copy-done.8) | copy-start | bytes 3538948
  265.8 3.9 copy-start.27
  269.7 199.8 %copy-start.23 = (f32[2,128]{1,0:T(2,128)S(1)}, f32[2,128]{1,0:T(2,128)}, u32[]{:S(2)}) copy-start(f32[2,128]{1,0:T(2,128)} %get-tuple-element.729) | copy-start | bytes 3076
  269.7 199.8 %copy-start.24 = (f32[1,2]{1,0:T(1,128)S(1)}, f32[1,2]{1,0:T(1,128)}, u32[]{:S(2)}) copy-start(f32[1,2]{1,0:T(1,128)} %param.45) | copy-start | bytes 28
  269.7 5.2 copy-start.4
  368.0 1.6 copy-start.5
  369.6 5.1 copy-start.4
  467.8 1.6 copy-start.5
  469.5 47.9 %copy-start.1 = (bf16[1,2,128,2048]{3,2,1,0:T(8,128)(2,1)S(1)}, bf16[1,2,128,2048]{3,2,1,0:T(8,128)(2,1)}, u32[]{:S(2)}) copy-start(bf16[1,2,128,2048]{3,2,1,0:T(8,128)(2,1)} %param.39) | copy-start | bytes 3145732
  469.5 47.9 %copy-start.3 = (bf16[2,18,128,128]{3,2,1,0:T(8,128)(2,1)S(1)}, bf16[2,18,128,128]{3,2,1,0:T(8,128)(2,1)}, u32[]{:S(2)}) copy-start(bf16[2,18,128,128]{3,2,1,0:T(8,128)(2,1)} %get-tuple-element.728) | copy-start | bytes 3538948
  524.6 1.7 copy-start.20
  526.3 7.2 %copy-start.14 = (bf16[2,4,128,128]{2,3,1,0:T(8,128)(2,1)S(1)}, bf16[2,4,128,128]{2,3,1,0:T(8,128)(2,1)}, u32[]{:S(2)}) copy-start(bf16[2,4,128,128]{2,3,1,0:T(8,128)(2,1)} %get-tuple-element.1133) | copy-start | bytes 786436 | tf_op jit(solution)/shard_map/cond/branch_1_fun/while
  535.3 1.7 copy-start.20
  537.1 7.2 %copy-start.14 = (bf16[2,4,128,128]{2,3,1,0:T(8,128)(2,1)S(1)}, bf16[2,4,128,128]{2,3,1,0:T(8,128)(2,1)}, u32[]{:S(2)}) copy-start(bf16[2,4,128,128]{2,3,1,0:T(8,128)(2,1)} %get-tuple-element.1133) | copy-start | bytes 786436 | tf_op jit(solution)/shard_map/cond/branch_1_fun/while
  548.0 7.2 %copy-start.11 = (bf16[2,4,128,128]{2,3,1,0:T(8,128)(2,1)S(1)}, bf16[2,4,128,128]{2,3,1,0:T(8,128)(2,1)}, u32[]{:S(2)}) copy-start(bf16[2,4,128,128]{2,3,1,0:T(8,128)(2,1)} %get-tuple-element.1151) | copy-start | bytes 786436 | tf_op jit(solution)/shard_map/cond/branch_1_fun/while
  558.6 7.2 %copy-start.11 = (bf16[2,4,128,128]{2,3,1,0:T(8,128)(2,1)S(1)}, bf16[2,4,128,128]{2,3,1,0:T(8,128)(2,1)}, u32[]{:S(2)}) copy-start(bf16[2,4,128,128]{2,3,1,0:T(8,128)(2,1)} %get-tuple-element.1151) | copy-start | bytes 786436 | tf_op jit(solution)/shard_map/cond/branch_1_fun/while
Sparse Core Ops, SparseCore 0:
  11.7 112.4 all-gather.2
